TPU v7x, 128 devices: a whole 4x4x4 slice. The times are simulated.
128 devices in a mesh: leaf: 16 (over x_lo, y, core), grid: 8 (over x_hi, z).
Axes of the slice: x: 4 (x_hi: 2, x_lo: 2; x = x_hi * 2 + x_lo), y: 4, z: 4, core: 2. Of those that a mesh axis runs over, the one named last changes fastest.
Arguments:
- child_front: float32 [16, 1, 2048, 2, 8, 128], P('leaf', None, None, None, 'grid'), as said below
- child_live: int32 [16, 1, 16], replicated, may hold values 0 or 1
- child_map: int32 [16, 1, 8], replicated, may hold values from 0 to 15, as said below
- parent_owner: int32 [8, 16], replicated, may hold values from 0 to 15, as said below
- parent_shift: float32 [16, 1, 1, 8, 128], P('leaf', None, None, 'grid'), may hold values from 0.5 to 2
Outputs:
- child_factor: float32 [16, 1, 2048, 1, 8, 128], P('leaf', None, None, None, 'grid')
- parent_done: float32 [16, 1, 2048, 1, 8, 128], P('leaf', None, None, None, 'grid')
Inputs may be any that keep to these rules, and one draw needn't show every extreme that they name: `child_map`: each row holds 8 different block numbers in increasing order, the last one being 15. `parent_owner`: each row is a permutation of the 16 slots. `child_front`: each front is symmetric positive definite.
All inputs are finite; a program needn't handle non-finite values.
Results may differ from a plain program's by a relative error of at most 0.0003.
Values sent between devices are 32-bit elements; how exact they have to be, the bound alone decides.
No kernel may reach another device: no remote copies, remote signals or barrier semaphores. Data moves between devices by JAX's collectives and lax.ppermute only.
A program may use at most 128 MiB of HBM per device.

v0:
```python
import jax
import jax.numpy as jnp
from jax import lax
from jax.sharding import PartitionSpec as P

F = 2048
PIVOTS = 1024
NB = 128
CORDER = 1024
FB = 16
PB = 8
CB = 8
highest = lax.Precision.HIGHEST


def broadcast(value, axis, root):
    mine = lax.axis_index(axis) == root
    return lax.psum(jnp.where(mine, value, jnp.zeros_like(value)), axis)


def swapped_2(value, axis, distance):
    mask = 2**distance
    pairs = [(source, source ^ mask) for source in range(lax.axis_size(axis))]
    return lax.ppermute(value, axis, pairs)


def panel_factor(column_tail):
    lower_part = jnp.linalg.cholesky(column_tail[:, :NB])
    below_part = lax.linalg.triangular_solve(
        lower_part, column_tail[:, NB:], left_side=False, lower=True, transpose_a=True
    )
    return jnp.concatenate([lower_part, below_part], axis=1)


def apply_panel(front_cols, panel_cols, block_ids, panel):
    first_row = panel * NB
    pieces = []
    for round_pick in range(front_cols.shape[2]):
        target = block_ids[round_pick]
        offset = jnp.clip(target * NB - first_row, 0, F - first_row - NB)
        partner = lax.dynamic_slice_in_dim(panel_cols, offset, NB, 1)
        change = jnp.einsum("frn,fsn->frs", panel_cols, partner, precision=highest)
        current = front_cols[:, first_row:, round_pick, :]
        updated = jnp.where(target > panel, current - change, current)
        updated = jnp.where(target == panel, panel_cols, updated)
        upper_rows = jnp.where(target == panel, 0.0, front_cols[:, :first_row, round_pick, :])
        pieces.append(jnp.concatenate([upper_rows, updated], axis=1))
    return jnp.stack(pieces, axis=2)


def mask_front(front_cols, alive_mask, block_ids):
    live_rows = jnp.repeat(alive_mask, NB, axis=1)
    choose = (jnp.arange(FB)[:, None] == block_ids[None, :]).astype(jnp.float32)
    live_cols = jnp.dot(alive_mask, choose, precision=highest)
    places = block_ids[:, None] * NB + jnp.arange(NB)[None, :]
    diagonal = (jnp.arange(F)[:, None, None] == places[None]).astype(jnp.float32)
    kept = front_cols * live_rows[:, :, None, None] * live_cols[:, None, :, None]
    return kept + diagonal[None] * (1.0 - live_cols)[:, None, :, None]


def place_column(schur, targets, alive_mask, target):
    fronts = schur.shape[0]
    pick = (targets == target).astype(jnp.float32) * alive_mask
    tiles = schur.reshape(fronts, CORDER, CB, NB)
    column = jnp.einsum("fc,frcj->frj", pick, tiles, precision=highest)
    spread = (targets[:, None, :] == jnp.arange(FB)[None, :, None]).astype(
        jnp.float32
    ) * alive_mask[:, None, :]
    placed = jnp.einsum(
        "fbc,fcij->fbij", spread, column.reshape(fronts, CB, NB, NB), precision=highest
    )
    return placed.reshape(fronts, F, NB)


def body(child_front, child_live, child_map, parent_owner, parent_shift):
    grid_count = lax.axis_size("grid")
    grid_pos = lax.axis_index("grid")
    leaf_pos = lax.axis_index("leaf")
    member = leaf_pos % 2
    pair = leaf_pos // 2
    sibling = leaf_pos ^ 1
    fronts = child_front.shape[1]
    child_rounds = child_front.shape[3]
    pivot_rounds = PIVOTS // (NB * grid_count)
    parent_rounds = parent_shift.shape[2]
    my_alive = lax.dynamic_index_in_dim(child_live, leaf_pos, 0, keepdims=False).astype(jnp.float32)
    other_alive = lax.dynamic_index_in_dim(child_live, sibling, 0, keepdims=False).astype(
        jnp.float32
    )
    my_map = lax.dynamic_index_in_dim(child_map, leaf_pos, 0, keepdims=False)
    other_map = lax.dynamic_index_in_dim(child_map, sibling, 0, keepdims=False)
    child_blocks = jnp.arange(child_rounds) * grid_count + grid_pos
    front_cols = mask_front(
        child_front.reshape(fronts, F, child_rounds, NB), my_alive, child_blocks
    )
    for panel in range(PB):
        column = front_cols[:, :, panel // grid_count, :]
        outgoing = column
        arrived = broadcast(outgoing, "grid", panel % grid_count)
        column_tail = arrived[:, panel * NB :]
        front_cols = apply_panel(front_cols, panel_factor(column_tail), child_blocks, panel)
    child_factor = front_cols[:, :, :pivot_rounds, :]
    contrib = front_cols[:, PIVOTS:, pivot_rounds:, :]
    gathered = lax.all_gather(contrib[:, :, :, None, :], "grid", axis=3, tiled=True)
    mine_schur = gathered.reshape(fronts, CORDER, CORDER)
    other_schur = swapped_2(mine_schur, "leaf", 0)
    owner_row = lax.dynamic_index_in_dim(parent_owner, pair, 0, keepdims=False)
    slot_ids = (member * grid_count + grid_pos) * parent_rounds + jnp.arange(parent_rounds)
    holders = (owner_row[:, None] == slot_ids[None, :]).astype(jnp.int32)
    parent_blocks = jnp.sum(holders * jnp.arange(FB)[:, None], axis=0)
    shift_cols = parent_shift.reshape(fronts, parent_rounds, NB)
    my_live_contrib = my_alive[:, PB:]
    other_live_contrib = other_alive[:, PB:]
    target = parent_blocks[0]
    column = place_column(mine_schur, my_map, my_live_contrib, target)
    column = column + place_column(other_schur, other_map, other_live_contrib, target)
    places = target * NB + jnp.arange(NB)
    diagonal = (jnp.arange(F)[:, None] == places[None, :]).astype(jnp.float32)
    pieces = [column + diagonal[None] * shift_cols[:, 0, None, :]]
    parent_cols = jnp.stack(pieces, axis=2)
    for panel in range(PB):
        holder = owner_row[panel]
        holder_side = holder // (grid_count * parent_rounds)
        holder_grid = holder // parent_rounds % grid_count
        holder_round = holder % parent_rounds
        column = lax.dynamic_index_in_dim(parent_cols, holder_round, 2, keepdims=False)
        outgoing = column
        arrived = broadcast(outgoing, "grid", holder_grid)
        swapped = swapped_2(arrived, "leaf", 0)
        received = jnp.where(member == holder_side, arrived, swapped)
        column_tail = received[:, panel * NB :]
        parent_cols = apply_panel(parent_cols, panel_factor(column_tail), parent_blocks, panel)
    upper_part = (jnp.arange(F) < PIVOTS)[None, :, None, None] & (parent_blocks >= PB)[
        None, None, :, None
    ]
    parent_cols = jnp.where(upper_part, 0.0, parent_cols)
    return (
        child_factor.reshape(1, fronts, F, pivot_rounds, 1, NB),
        parent_cols.reshape(1, fronts, F, parent_rounds, 1, NB),
    )


def solution(mesh):
    in_specs = (
        P("leaf", None, None, None, "grid", None),
        P(),
        P(),
        P(),
        P("leaf", None, None, "grid", None),
    )
    out_specs = (
        P("leaf", None, None, None, "grid", None),
        P("leaf", None, None, None, "grid", None),
    )
    return jax.shard_map(body, mesh=mesh, in_specs=in_specs, out_specs=out_specs, check_vma=False)
```

profile of v0, /device:TPU:1, one launch (start us, length us, event | category | flops | bytes accessed | tf_op | source)
XLA Modules:
  0.0 2009.4 jit_solution(2481067446718470726)
XLA Ops:
  19.1 83.7 %all-reduce.17.cloned.1.call-done = f32[1,2048,128]{1,2,0:T(8,128)} async-done(((f32[1,2048,128]{1,2,0:T(8,128)}), f32[1,2048,128]{1,2,0:T(8,128)}) %all-reduce.17.cloned.1.call-update) | async-done | bytes 1048592 | tf_op jit(solution)/shard_map/psum | solution.py:18
  104.7 11.7 custom-call.50
  135.0 84.5 %all-reduce.19.cloned.1.call-done = f32[1,2048,128]{1,2,0:T(8,128)} async-done(((f32[1,2048,128]{1,2,0:T(8,128)}), f32[1,2048,128]{1,2,0:T(8,128)}) %all-reduce.19.cloned.1.call-update) | async-done | bytes 1048592 | tf_op jit(solution)/shard_map/psum | solution.py:18
  221.3 11.7 custom-call.52
  250.7 84.3 %all-reduce.21.cloned.1.call-done = f32[1,2048,128]{1,2,0:T(8,128)} async-done(((f32[1,2048,128]{1,2,0:T(8,128)}), f32[1,2048,128]{1,2,0:T(8,128)}) %all-reduce.21.cloned.1.call-update) | async-done | bytes 1048592 | tf_op jit(solution)/shard_map/psum | solution.py:18
  336.7 11.7 custom-call.54
  386.0 64.7 %all-reduce.23.cloned.1.call-done = f32[1,2048,128]{1,2,0:T(8,128)} async-done(((f32[1,2048,128]{1,2,0:T(8,128)}), f32[1,2048,128]{1,2,0:T(8,128)}) %all-reduce.23.cloned.1.call-update) | async-done | bytes 1048592 | tf_op jit(solution)/shard_map/psum | solution.py:18
  452.5 11.7 custom-call.56
  483.9 82.4 %all-reduce.25.cloned.1.call-done = f32[1,2048,128]{1,2,0:T(8,128)} async-done(((f32[1,2048,128]{1,2,0:T(8,128)}), f32[1,2048,128]{1,2,0:T(8,128)}) %all-reduce.25.cloned.1.call-update) | async-done | bytes 1048592 | tf_op jit(solution)/shard_map/psum | solution.py:18
  568.1 11.7 custom-call.58
  599.9 82.9 %all-reduce.27.cloned.1.call-done = f32[1,2048,128]{1,2,0:T(8,128)} async-done(((f32[1,2048,128]{1,2,0:T(8,128)}), f32[1,2048,128]{1,2,0:T(8,128)}) %all-reduce.27.cloned.1.call-update) | async-done | bytes 1048592 | tf_op jit(solution)/shard_map/psum | solution.py:18
  684.5 11.7 custom-call.60
  715.0 82.7 %all-reduce.29.cloned.1.call-done = f32[1,2048,128]{1,2,0:T(8,128)} async-done(((f32[1,2048,128]{1,2,0:T(8,128)}), f32[1,2048,128]{1,2,0:T(8,128)}) %all-reduce.29.cloned.1.call-update) | async-done | bytes 1048592 | tf_op jit(solution)/shard_map/psum | solution.py:18
  799.4 11.7 custom-call.62
  828.1 84.6 %all-reduce.31.cloned.1.call-done = f32[1,2048,128]{1,2,0:T(8,128)} async-done(((f32[1,2048,128]{1,2,0:T(8,128)}), f32[1,2048,128]{1,2,0:T(8,128)}) %all-reduce.31.cloned.1.call-update) | async-done | bytes 1048592 | tf_op jit(solution)/shard_map/psum | solution.py:18
  941.4 74.2 %all-gather.3.cloned.1.call-done = f32[1,1024,8,128]{3,1,0,2:T(8,128)} async-done(((f32[1,1024,1,128]{3,1,0,2:T(8,128)}), f32[1,1024,8,128]{3,1,0,2:T(8,128)}) %all-gather.3.cloned.1.call-update) | async-done | bytes 4194320 | tf_op jit(solution)/shard_map/all_gather | solution.py:104
  1054.6 80.3 %all-reduce.33.cloned.1.call-done = f32[1,2048,128]{1,2,0:T(8,128)} async-done(((f32[1,2048,128]{1,2,0:T(8,128)}), f32[1,2048,128]{1,2,0:T(8,128)}) %all-reduce.33.cloned.1.call-update) | async-done | bytes 1048592 | tf_op jit(solution)/shard_map/psum | solution.py:18
  1172.9 80.5 %all-reduce.35.cloned.1.call-done = f32[1,2048,128]{1,2,0:T(8,128)} async-done(((f32[1,2048,128]{1,2,0:T(8,128)}), f32[1,2048,128]{1,2,0:T(8,128)}) %all-reduce.35.cloned.1.call-update) | async-done | bytes 1048592 | tf_op jit(solution)/shard_map/psum | solution.py:18
  1291.3 80.5 %all-reduce.37.cloned.1.call-done = f32[1,2048,128]{1,2,0:T(8,128)} async-done(((f32[1,2048,128]{1,2,0:T(8,128)}), f32[1,2048,128]{1,2,0:T(8,128)}) %all-reduce.37.cloned.1.call-update) | async-done | bytes 1048592 | tf_op jit(solution)/shard_map/psum | solution.py:18
  1409.3 80.4 %all-reduce.39.cloned.1.call-done = f32[1,2048,128]{1,2,0:T(8,128)} async-done(((f32[1,2048,128]{1,2,0:T(8,128)}), f32[1,2048,128]{1,2,0:T(8,128)}) %all-reduce.39.cloned.1.call-update) | async-done | bytes 1048592 | tf_op jit(solution)/shard_map/psum | solution.py:18
  1527.5 80.5 %all-reduce.41.cloned.1.call-done = f32[1,2048,128]{1,2,0:T(8,128)} async-done(((f32[1,2048,128]{1,2,0:T(8,128)}), f32[1,2048,128]{1,2,0:T(8,128)}) %all-reduce.41.cloned.1.call-update) | async-done | bytes 1048592 | tf_op jit(solution)/shard_map/psum | solution.py:18
  1645.4 80.4 %all-reduce.43.cloned.1.call-done = f32[1,2048,128]{1,2,0:T(8,128)} async-done(((f32[1,2048,128]{1,2,0:T(8,128)}), f32[1,2048,128]{1,2,0:T(8,128)}) %all-reduce.43.cloned.1.call-update) | async-done | bytes 1048592 | tf_op jit(solution)/shard_map/psum | solution.py:18
  1763.4 80.5 %all-reduce.45.cloned.1.call-done = f32[1,2048,128]{1,2,0:T(8,128)} async-done(((f32[1,2048,128]{1,2,0:T(8,128)}), f32[1,2048,128]{1,2,0:T(8,128)}) %all-reduce.45.cloned.1.call-update) | async-done | bytes 1048592 | tf_op jit(solution)/shard_map/psum | solution.py:18
  1881.2 80.5 %all-reduce.47.cloned.1.call-done = f32[1,2048,128]{1,2,0:T(8,128)} async-done(((f32[1,2048,128]{1,2,0:T(8,128)}), f32[1,2048,128]{1,2,0:T(8,128)}) %all-reduce.47.cloned.1.call-update) | async-done | bytes 1048592 | tf_op jit(solution)/shard_map/psum | solution.py:18
  (345 shorter events, 490.2 us)
Async XLA Ops:
  7.2 95.7 %all-reduce.17.cloned.1.call-start = ((), (), s32[]{:S(2)}) async-start(), calls=%async_computation | async-start | bytes 2097152 | tf_op jit(solution)/shard_map/psum | solution.py:18
  16.6 202.9 %all-reduce.19.cloned.1.call-start = ((), (), s32[]{:S(2)}) async-start(), calls=%async_computation.1 | async-start | bytes 2097152 | tf_op jit(solution)/shard_map/psum | solution.py:18
  133.5 201.4 %all-reduce.21.cloned.1.call-start = ((), (), s32[]{:S(2)}) async-start(), calls=%async_computation.2 | async-start | bytes 2097152 | tf_op jit(solution)/shard_map/psum | solution.py:18
  249.0 201.7 %all-reduce.23.cloned.1.call-start = ((), (), s32[]{:S(2)}) async-start(), calls=%async_computation.3 | async-start | bytes 2097152 | tf_op jit(solution)/shard_map/psum | solution.py:18
  364.7 201.6 %all-reduce.25.cloned.1.call-start = ((), (), s32[]{:S(2)}) async-start(), calls=%async_computation.4 | async-start | bytes 2097152 | tf_op jit(solution)/shard_map/psum | solution.py:18
  480.2 202.5 %all-reduce.27.cloned.1.call-start = ((), (), s32[]{:S(2)}) async-start(), calls=%async_computation.5 | async-start | bytes 2097152 | tf_op jit(solution)/shard_map/psum | solution.py:18
  596.8 200.9 %all-reduce.29.cloned.1.call-start = ((), (), s32[]{:S(2)}) async-start(), calls=%async_computation.6 | async-start | bytes 2097152 | tf_op jit(solution)/shard_map/psum | solution.py:18
  711.6 201.1 %all-reduce.31.cloned.1.call-start = ((), (), s32[]{:S(2)}) async-start(), calls=%async_computation.7 | async-start | bytes 2097152 | tf_op jit(solution)/shard_map/psum | solution.py:18
  826.7 188.8 %all-gather.3.cloned.1.call-start = ((), (), s32[]{:S(2)}) async-start(), calls=%async_computation.16 | async-start | bytes 4718592 | tf_op jit(solution)/shard_map/all_gather | solution.py:104
  941.3 193.6 %all-reduce.33.cloned.1.call-start = ((), (), s32[]{:S(2)}) async-start(), calls=%async_computation.8 | async-start | bytes 2097152 | tf_op jit(solution)/shard_map/psum | solution.py:18
  1020.9 16.3 collective-permute-start
  1054.6 198.8 %all-reduce.35.cloned.1.call-start = ((), (), s32[]{:S(2)}) async-start(), calls=%async_computation.9 | async-start | bytes 2097152 | tf_op jit(solution)/shard_map/psum | solution.py:18
  1172.8 199.0 %all-reduce.37.cloned.1.call-start = ((), (), s32[]{:S(2)}) async-start(), calls=%async_computation.10 | async-start | bytes 2097152 | tf_op jit(solution)/shard_map/psum | solution.py:18
  1253.3 10.0 collective-permute-start.2
  1291.3 198.5 %all-reduce.39.cloned.1.call-start = ((), (), s32[]{:S(2)}) async-start(), calls=%async_computation.11 | async-start | bytes 2097152 | tf_op jit(solution)/shard_map/psum | solution.py:18
  1409.3 198.7 %all-reduce.41.cloned.1.call-start = ((), (), s32[]{:S(2)}) async-start(), calls=%async_computation.12 | async-start | bytes 2097152 | tf_op jit(solution)/shard_map/psum | solution.py:18
  1489.7 10.0 collective-permute-start.4
  1527.4 198.4 %all-reduce.43.cloned.1.call-start = ((), (), s32[]{:S(2)}) async-start(), calls=%async_computation.13 | async-start | bytes 2097152 | tf_op jit(solution)/shard_map/psum | solution.py:18
  1608.0 9.8 collective-permute-start.5
  1645.4 198.5 %all-reduce.45.cloned.1.call-start = ((), (), s32[]{:S(2)}) async-start(), calls=%async_computation.14 | async-start | bytes 2097152 | tf_op jit(solution)/shard_map/psum | solution.py:18
  1725.8 10.0 collective-permute-start.6
  1763.4 198.3 %all-reduce.47.cloned.1.call-start = ((), (), s32[]{:S(2)}) async-start(), calls=%async_computation.15 | async-start | bytes 2097152 | tf_op jit(solution)/shard_map/psum | solution.py:18
  1843.9 9.9 collective-permute-start.7
  1961.7 12.7 collective-permute-start.8
  (11 other events, 398.2 us)
Sparse Core Ops, SparseCore 0:
  16.7 86.0 all-reduce.16
  133.6 85.8 all-reduce.18
  249.1 85.8 all-reduce.20
  364.8 85.8 all-reduce.22
  480.3 85.8 all-reduce.24
  596.9 85.8 all-reduce.26
  711.8 85.8 all-reduce.28
  826.9 85.8 all-reduce.30
  941.4 74.1 all-gather.2
  1054.7 80.1 all-reduce.32
  1172.9 80.3 all-reduce.34
  1291.4 80.3 all-reduce.36
  1409.4 80.3 all-reduce.38
  1527.6 80.3 all-reduce.40
  1645.5 80.3 all-reduce.42
  1763.5 80.3 all-reduce.44
  1881.3 80.3 all-reduce.46
where the time goes:
time: 2020 us; the launch traced here: 2010 us
  waiting for transfers between devices  1370 us (68%)
  other arithmetic  413 us (20%)
  between operations  69.7 us (3%)
  matrix products  69.2 us (3%)
  starting transfers between devices  51 us (3%)
  local copies, waits for them, and re-layouts  38.3 us (2%)
    psum x16, waiting for transfers between devices, broadcast(): return lax.psum(jnp.where(mine, value, jnp.zeros_like(value)), axis)  1290 us
    another operation x48, other arithmetic, panel_factor(): lower_part = jnp.linalg.cholesky(column_tail[:, :NB])  199 us
    another operation x32, other arithmetic, panel_factor(): lax.linalg.triangular_solve(lower_part, column_tail[:, NB:], left_side=Fa...  168 us
    all_gather x1, waiting for transfers between devices, body(): lax.all_gather(contrib[:, :, :, None, :], 'grid', axis=3, tiled=True)  74.2 us
    ppermute x9, starting transfers between devices, swapped_2(): return lax.ppermute(value, axis, pairs)  48.5 us
  transfers between devices with their start and end apart: 26, of which 17 were waited for; matrix products, arithmetic and copies ran while one was open for 2% of the time, Pallas kernels for 0%

commit v1 on v0

--- a/solution.py
+++ b/solution.py
@@ -15,7 +15,7 @@
 
 def broadcast(value, axis, root):
     mine = lax.axis_index(axis) == root
-    return lax.psum(jnp.where(mine, value, jnp.zeros_like(value)), axis)
+    return jnp.sum(lax.all_gather(jnp.where(mine, value, jnp.zeros_like(value)), axis), axis=0)
 
 
 def swapped_2(value, axis, distance):

time: 2020 us -> 2540 us (1.26)
  waiting for transfers between devices: 1370 us -> 1700 us
  local copies, waits for them, and re-layouts: 38.3 us -> 143 us
  other arithmetic: 413 us -> 511 us
  starting transfers between devices: 51 us -> 14.2 us
    all_gather x0 -> x16, waiting for transfers between devices: none -> 1630 us  [broadcast(): lax.all_gather(jnp.where(mine, value, jnp.zeros_like(value)), axis)]
    psum x16 -> x0, waiting for transfers between devices: 1290 us -> none  [broadcast(): return lax.psum(jnp.where(mine, value, jnp.zeros_like(value)), axis)]
    reduce_sum x0 -> x16, other arithmetic: none -> 64.6 us  [broadcast(): jnp.sum(lax.all_gather(jnp.where(mine, value, jnp.zeros_like(value)), axi...]
    ppermute x9, starting transfers between devices: 48.5 us -> 11.8 us  [swapped_2(): return lax.ppermute(value, axis, pairs)]
    unnamed x21 -> x109, local copies, waits for them, and re-layouts: 11.2 us -> 41.9 us
    select_n x0 -> x14, local copies, waits for them, and re-layouts: none -> 28.1 us  [broadcast(): jnp.where(mine, value, jnp.zeros_like(value))]
where the time goes in v1:
time: 2540 us; the launch traced here: 2520 us
  waiting for transfers between devices  1700 us (67%)
  other arithmetic  511 us (20%)
  local copies, waits for them, and re-layouts  143 us (6%)
  matrix products  87.6 us (3%)
  between operations  69.6 us (3%)
    all_gather x16, waiting for transfers between devices, broadcast(): lax.all_gather(jnp.where(mine, value, jnp.zeros_like(value)), axis)  1630 us
    another operation x48, other arithmetic, panel_factor(): lower_part = jnp.linalg.cholesky(column_tail[:, :NB])  206 us
    another operation x32, other arithmetic, panel_factor(): lax.linalg.triangular_solve(lower_part, column_tail[:, NB:], left_side=Fa...  179 us
    all_gather x1, waiting for transfers between devices, body(): lax.all_gather(contrib[:, :, :, None, :], 'grid', axis=3, tiled=True)  69.4 us
    reduce_sum x16, other arithmetic, broadcast(): jnp.sum(lax.all_gather(jnp.where(mine, value, jnp.zeros_like(value)), axi...  64.6 us
  transfers between devices with their start and end apart: 26, of which 17 were waited for; matrix products, arithmetic and copies ran while one was open for 2% of the time, Pallas kernels for 0%

profile of v1, /device:TPU:1, one launch (start us, length us, event | category | flops | bytes accessed | tf_op | source)
XLA Modules:
  0.0 2522.6 jit_solution(5092807209873915012)
XLA Ops:
  23.5 107.6 %all-gather.48.cloned.1.call-done = f32[8,2048,1,128]{3,1,2,0:T(8,128)} async-done(((f32[1,2048,1,128]{3,1,2,0:T(8,128)}), f32[8,2048,1,128]{3,1,2,0:T(8,128)}) %all-gather.48.cloned.1.call-update) | async-done | bytes 8388624 | tf_op jit(solution)/shard_map/all_gather | solution.py:18
  140.3 11.7 custom-call.50
  170.5 102.8 %all-gather.50.cloned.1.call-done = f32[16384,128]{0,1:T(8,128)} async-done(((f32[2048,128]{0,1:T(8,128)}), f32[16384,128]{0,1:T(8,128)}) %all-gather.50.cloned.1.call-update) | async-done | bytes 8388624 | tf_op jit(solution)/shard_map/all_gather | solution.py:18
  285.5 11.9 custom-call.52
  318.1 102.8 %all-gather.22.cloned.1.call-done = f32[8,1,2048,128]{3,2,1,0:T(8,128)} async-done(((f32[1,1,2048,128]{3,2,1,0:T(8,128)}), f32[8,1,2048,128]{3,2,1,0:T(8,128)}) %all-gather.22.cloned.1.call-update) | async-done | bytes 8388624 | tf_op jit(solution)/shard_map/all_gather | solution.py:18
  427.8 11.7 custom-call.54
  464.5 100.4 %all-gather.24.cloned.1.call-done = f32[8,1,2048,128]{3,2,1,0:T(8,128)} async-done(((f32[1,1,2048,128]{3,2,1,0:T(8,128)}), f32[8,1,2048,128]{3,2,1,0:T(8,128)}) %all-gather.24.cloned.1.call-update) | async-done | bytes 8388624 | tf_op jit(solution)/shard_map/all_gather | solution.py:18
  614.8 100.5 %all-gather.26.cloned.1.call-done = f32[8,1,2048,128]{3,2,1,0:T(8,128)} async-done(((f32[1,1,2048,128]{3,2,1,0:T(8,128)}), f32[8,1,2048,128]{3,2,1,0:T(8,128)}) %all-gather.26.cloned.1.call-update) | async-done | bytes 8388624 | tf_op jit(solution)/shard_map/all_gather | solution.py:18
  727.3 13.2 custom-call.58
  774.1 100.5 %all-gather.28.cloned.1.call-done = f32[8,1,2048,128]{3,2,1,0:T(8,128)} async-done(((f32[1,1,2048,128]{3,2,1,0:T(8,128)}), f32[8,1,2048,128]{3,2,1,0:T(8,128)}) %all-gather.28.cloned.1.call-update) | async-done | bytes 8388624 | tf_op jit(solution)/shard_map/all_gather | solution.py:18
  886.6 13.2 custom-call.60
  933.5 100.2 %all-gather.30.cloned.1.call-done = f32[8,1,2048,128]{3,2,1,0:T(8,128)} async-done(((f32[1,1,2048,128]{3,2,1,0:T(8,128)}), f32[8,1,2048,128]{3,2,1,0:T(8,128)}) %all-gather.30.cloned.1.call-update) | async-done | bytes 8388624 | tf_op jit(solution)/shard_map/all_gather | solution.py:18
  1045.7 13.2 custom-call.62
  1109.4 83.1 %all-gather.32.cloned.1.call-done = f32[8,1,2048,128]{3,2,1,0:T(8,128)} async-done(((f32[1,1,2048,128]{3,2,1,0:T(8,128)}), f32[8,1,2048,128]{3,2,1,0:T(8,128)}) %all-gather.32.cloned.1.call-update) | async-done | bytes 8388624 | tf_op jit(solution)/shard_map/all_gather | solution.py:18
  1196.9 11.9 custom-call.64
  1222.8 69.4 %all-gather.52.cloned.1.call-done = f32[1,1024,8,128]{3,1,0,2:T(8,128)} async-done(((f32[1,1024,1,128]{3,1,0,2:T(8,128)}), f32[1,1024,8,128]{3,1,0,2:T(8,128)}) %all-gather.52.cloned.1.call-update) | async-done | bytes 4194320 | tf_op jit(solution)/shard_map/all_gather | solution.py:104
  1335.6 104.2 %all-gather.34.cloned.1.call-done = f32[8,1,2048,128]{3,2,1,0:T(8,128)} async-done(((f32[1,1,2048,128]{3,2,1,0:T(8,128)}), f32[8,1,2048,128]{3,2,1,0:T(8,128)}) %all-gather.34.cloned.1.call-update) | async-done | bytes 8388624 | tf_op jit(solution)/shard_map/all_gather | solution.py:18
  1483.8 104.3 %all-gather.54.cloned.1.call-done = f32[16384,128]{0,1:T(8,128)} async-done(((f32[2048,128]{0,1:T(8,128)}), f32[16384,128]{0,1:T(8,128)}) %all-gather.54.cloned.1.call-update) | async-done | bytes 8388624 | tf_op jit(solution)/shard_map/all_gather | solution.py:18
  1639.9 104.1 %all-gather.36.cloned.1.call-done = f32[8,1,2048,128]{3,2,1,0:T(8,128)} async-done(((f32[1,1,2048,128]{3,2,1,0:T(8,128)}), f32[8,1,2048,128]{3,2,1,0:T(8,128)}) %all-gather.36.cloned.1.call-update) | async-done | bytes 8388624 | tf_op jit(solution)/shard_map/all_gather | solution.py:18
  1787.9 104.2 %all-gather.38.cloned.1.call-done = f32[8,1,2048,128]{3,2,1,0:T(8,128)} async-done(((f32[1,1,2048,128]{3,2,1,0:T(8,128)}), f32[8,1,2048,128]{3,2,1,0:T(8,128)}) %all-gather.38.cloned.1.call-update) | async-done | bytes 8388624 | tf_op jit(solution)/shard_map/all_gather | solution.py:18
  1933.0 104.5 %all-gather.40.cloned.1.call-done = f32[8,1,2048,128]{3,2,1,0:T(8,128)} async-done(((f32[1,1,2048,128]{3,2,1,0:T(8,128)}), f32[8,1,2048,128]{3,2,1,0:T(8,128)}) %all-gather.40.cloned.1.call-update) | async-done | bytes 8388624 | tf_op jit(solution)/shard_map/all_gather | solution.py:18
  2079.2 104.4 %all-gather.42.cloned.1.call-done = f32[8,1,2048,128]{3,2,1,0:T(8,128)} async-done(((f32[1,1,2048,128]{3,2,1,0:T(8,128)}), f32[8,1,2048,128]{3,2,1,0:T(8,128)}) %all-gather.42.cloned.1.call-update) | async-done | bytes 8388624 | tf_op jit(solution)/shard_map/all_gather | solution.py:18
  2223.6 104.2 %all-gather.44.cloned.1.call-done = f32[8,1,2048,128]{3,2,1,0:T(8,128)} async-done(((f32[1,1,2048,128]{3,2,1,0:T(8,128)}), f32[8,1,2048,128]{3,2,1,0:T(8,128)}) %all-gather.44.cloned.1.call-update) | async-done | bytes 8388624 | tf_op jit(solution)/shard_map/all_gather | solution.py:18
  2374.6 99.7 %all-gather.46.cloned.1.call-done = f32[8,1,2048,128]{3,2,1,0:T(8,128)} async-done(((f32[1,1,2048,128]{3,2,1,0:T(8,128)}), f32[8,1,2048,128]{3,2,1,0:T(8,128)}) %all-gather.46.cloned.1.call-update) | async-done | bytes 8388624 | tf_op jit(solution)/shard_map/all_gather | solution.py:18
  (487 shorter events, 669.4 us)
Async XLA Ops:
  7.2 124.0 %all-gather.48.cloned.1.call-start = ((), (), s32[]{:S(2)}) async-start(), calls=%async_computation.13 | async-start | bytes 9437184 | tf_op jit(solution)/shard_map/all_gather | solution.py:18
  20.9 252.4 %all-gather.50.cloned.1.call-start = ((), (), s32[]{:S(2)}) async-start(), calls=%async_computation.14 | async-start | bytes 9437184 | tf_op jit(solution)/shard_map/all_gather | solution.py:18
  168.2 252.7 %all-gather.22.cloned.1.call-start = ((), (), s32[]{:S(2)}) async-start(), calls=%async_computation | async-start | bytes 9437184 | tf_op jit(solution)/shard_map/all_gather | solution.py:18
  315.7 249.3 %all-gather.24.cloned.1.call-start = ((), (), s32[]{:S(2)}) async-start(), calls=%async_computation.1 | async-start | bytes 9437184 | tf_op jit(solution)/shard_map/all_gather | solution.py:18
  459.8 255.6 %all-gather.26.cloned.1.call-start = ((), (), s32[]{:S(2)}) async-start(), calls=%async_computation.2 | async-start | bytes 9437184 | tf_op jit(solution)/shard_map/all_gather | solution.py:18
  610.2 264.4 %all-gather.28.cloned.1.call-start = ((), (), s32[]{:S(2)}) async-start(), calls=%async_computation.3 | async-start | bytes 9437184 | tf_op jit(solution)/shard_map/all_gather | solution.py:18
  769.4 264.3 %all-gather.30.cloned.1.call-start = ((), (), s32[]{:S(2)}) async-start(), calls=%async_computation.4 | async-start | bytes 9437184 | tf_op jit(solution)/shard_map/all_gather | solution.py:18
  928.6 263.9 %all-gather.32.cloned.1.call-start = ((), (), s32[]{:S(2)}) async-start(), calls=%async_computation.5 | async-start | bytes 9437184 | tf_op jit(solution)/shard_map/all_gather | solution.py:18
  1087.3 204.9 %all-gather.52.cloned.1.call-start = ((), (), s32[]{:S(2)}) async-start(), calls=%async_computation.15 | async-start | bytes 4718592 | tf_op jit(solution)/shard_map/all_gather | solution.py:104
  1222.7 217.1 %all-gather.34.cloned.1.call-start = ((), (), s32[]{:S(2)}) async-start(), calls=%async_computation.6 | async-start | bytes 9437184 | tf_op jit(solution)/shard_map/all_gather | solution.py:18
  1297.5 16.1 collective-permute-start
  1335.6 252.5 %all-gather.54.cloned.1.call-start = ((), (), s32[]{:S(2)}) async-start(), calls=%async_computation.16 | async-start | bytes 9437184 | tf_op jit(solution)/shard_map/all_gather | solution.py:18
  1483.6 260.4 %all-gather.36.cloned.1.call-start = ((), (), s32[]{:S(2)}) async-start(), calls=%async_computation.7 | async-start | bytes 9437184 | tf_op jit(solution)/shard_map/all_gather | solution.py:18
  1600.1 5.7 collective-permute-start.2
  1639.8 252.2 %all-gather.38.cloned.1.call-start = ((), (), s32[]{:S(2)}) async-start(), calls=%async_computation.8 | async-start | bytes 9437184 | tf_op jit(solution)/shard_map/all_gather | solution.py:18
  1749.2 5.8 collective-permute-start.3
  1787.8 249.7 %all-gather.40.cloned.1.call-start = ((), (), s32[]{:S(2)}) async-start(), calls=%async_computation.9 | async-start | bytes 9437184 | tf_op jit(solution)/shard_map/all_gather | solution.py:18
  1897.2 5.9 collective-permute-start.4
  1932.9 250.6 %all-gather.42.cloned.1.call-start = ((), (), s32[]{:S(2)}) async-start(), calls=%async_computation.10 | async-start | bytes 9437184 | tf_op jit(solution)/shard_map/all_gather | solution.py:18
  2042.7 6.2 collective-permute-start.5
  2079.1 248.6 %all-gather.44.cloned.1.call-start = ((), (), s32[]{:S(2)}) async-start(), calls=%async_computation.11 | async-start | bytes 9437184 | tf_op jit(solution)/shard_map/all_gather | solution.py:18
  2223.5 250.8 %all-gather.46.cloned.1.call-start = ((), (), s32[]{:S(2)}) async-start(), calls=%async_computation.12 | async-start | bytes 9437184 | tf_op jit(solution)/shard_map/all_gather | solution.py:18
  2333.0 6.1 collective-permute-start.7
  2478.5 7.4 collective-permute-start.8
  (54 other events, 1331.5 us)
Sparse Core Ops, SparseCore 0:
  21.0 110.0 all-gather.47
  168.3 105.0 all-gather.49
  315.8 105.0 all-gather.21
  459.9 104.9 all-gather.23
  610.3 104.9 all-gather.25
  769.5 105.0 all-gather.27
  928.7 104.9 all-gather.29
  1087.4 104.9 all-gather.31
  1222.8 69.3 all-gather.51
  1335.7 104.0 all-gather.33
  1483.7 104.4 all-gather.53
  1639.9 103.9 all-gather.35
  1787.9 104.0 all-gather.37
  1933.0 104.4 all-gather.39
  2079.2 104.2 all-gather.41
  2223.6 104.0 all-gather.43
  2370.0 104.2 all-gather.45
